TPU v7x, 128 devices: a whole 4x4x4 slice. The times are simulated.
128 devices in a mesh: leaf: 4 (over y), row: 8 (over z, core), col: 4 (over x).
Axes of the slice: x: 4, y: 4, z: 4, core: 2. Of those that a mesh axis runs over, the one named last changes fastest.
Arguments:
- sigma_top: float32 [1024, 1024], P(('leaf', 'row'), 'col')
- panels: float32 [4, 7, 1024, 512], P('leaf', None, 'row', 'col'), may hold values from -0.1875 to 0.1875
- inverse_diag: float32 [4, 7, 512, 512], P('leaf', None, 'col')
- slot_lists: int32 [4, 6, 8], P('leaf'), may hold values from -1 to 11, as said below
- parent_links: int32 [4, 4], P('leaf'), may hold values from 1 to 2
Outputs:
- ancestor_block: float32 [4, 7, 1024, 512], P('leaf', None, 'row', 'col')
- diagonal_block: float32 [4, 7, 512, 512], P('leaf', None, None, 'col')
Inputs may be any that keep to these rules, and one draw needn't show every extreme that they name: `slot_lists`: in every row, entries 0 to 3 are 8 to 11 in order (the parent's own tiles); then come 1 to 3 distinct parent ancestor slots, below 8 for supernodes 1 and 2 and below 4 for supernodes 3 to 6; the rest are -1, so every row has padding. `parent_links`: each supernode 3 to 6 has supernode 1 or 2 as its parent. `sigma_top`: symmetric.
All inputs are finite; a program needn't handle non-finite values.
Results may differ from a plain program's by a relative error of at most 0.0001.
Values sent between devices are 32-bit elements; how exact they have to be, the bound alone decides.
A program may use at most 128 MiB of HBM per device.

v0:
```python
import jax
import jax.numpy as jnp
from jax import lax
from jax.sharding import PartitionSpec as P

TILE = 128
HIGHEST = lax.Precision.HIGHEST


def mm(a, b):
    return jnp.matmul(a, b, precision=HIGHEST, preferred_element_type=jnp.float32)


def tile_rows(matrix, index, tile):
    return lax.dynamic_slice_in_dim(matrix, index * tile, tile, 0)


def tile_cols(matrix, index, tile):
    return lax.dynamic_slice_in_dim(matrix, index * tile, tile, 1)


def scatter_factor(factor_col, slots, positions, tile):
    tiles = factor_col.reshape(slots.shape[0], tile, factor_col.shape[1])
    hits = slots[:, None] == jnp.arange(positions, dtype=slots.dtype)[None, :]
    present = jnp.any(hits, axis=0)
    source = jnp.argmax(hits, axis=0)
    moved = jnp.take(tiles, source, axis=0)
    moved = jnp.where(present[:, None, None], moved, 0.0)
    return moved.reshape(positions * tile, factor_col.shape[1])


def pick_transposed(column_block, picks, tile):
    tiles = column_block.reshape(-1, tile, tile)
    chosen = jnp.take(tiles, jnp.maximum(picks, 0), axis=0)
    chosen = jnp.where((picks >= 0)[:, None, None], chosen, 0.0)
    return jnp.transpose(chosen, (2, 0, 1)).reshape(tile, picks.shape[0] * tile)


def body(sigma_top, panels, inverse_diag, slot_lists, parent_links):
    tile = TILE
    row_count = lax.axis_size("row")
    col_count = lax.axis_size("col")
    leaf_count = lax.axis_size("leaf")
    r = lax.axis_index("row")
    c = lax.axis_index("col")
    panel = panels[0]
    inverse = inverse_diag[0]
    picks_all = slot_lists[0]
    parents = parent_links[0]
    nodes = panel.shape[0]
    width = inverse.shape[2]
    own_tiles = width // tile
    slot_count = picks_all.shape[1]
    positions = slot_count + own_tiles
    band = width // row_count
    partial_factor = mm(panel, inverse)
    factor_rows = lax.psum(partial_factor, "col")
    living = jnp.concatenate([jnp.ones((1, slot_count), jnp.bool_), picks_all >= 0], axis=0)
    live_here = jnp.take(living, r, axis=1).astype(jnp.float32)
    factor_rows = factor_rows * live_here[:, None, None]
    factor_tile = lax.dynamic_slice_in_dim(factor_rows, c * tile, tile, 2)
    factor_cols = lax.all_gather(factor_tile, "row", axis=1, tiled=True)
    inverse_band = lax.dynamic_slice_in_dim(inverse, r * band, band, 2)
    partial_gram = mm(jnp.transpose(inverse_band, (0, 2, 1)), inverse)
    gram_piece = lax.psum_scatter(partial_gram, "col", scatter_dimension=2, tiled=True)
    local_rows, local_cols = sigma_top.shape
    gathered = lax.all_gather(sigma_top, ("leaf", "row", "col"), axis=0)
    sigma = gathered.reshape(leaf_count * row_count, col_count, local_rows, local_cols)
    sigma = jnp.transpose(sigma, (0, 2, 1, 3)).reshape(
        leaf_count * row_count * local_rows, col_count * local_cols
    )

    def diag_partial(first, products):
        rows = factor_rows[first : first + products.shape[0]]
        return mm(jnp.transpose(rows, (0, 2, 1)), products)

    def reduce_and_gather(first, products):
        count = products.shape[0]
        piece = lax.psum_scatter(
            diag_partial(first, products), "row", scatter_dimension=1, tiled=True
        )
        piece = piece + gram_piece[first : first + count]
        both = jnp.concatenate([products, piece], axis=1)
        everything = lax.all_gather(both, ("row", "col"), axis=0)
        everything = everything.reshape(row_count, col_count, count, tile + band, tile)
        product_full = jnp.transpose(everything[:, :, :, :tile], (2, 0, 3, 1, 4)).reshape(
            count, row_count * tile, col_count * tile
        )
        diag_full = jnp.transpose(everything[:, :, :, tile:], (2, 0, 3, 1, 4)).reshape(
            count, row_count * band, col_count * tile
        )
        return (product_full, diag_full)

    own_row = jnp.minimum(r, own_tiles - 1)
    upper = r < own_tiles
    product_0 = mm(tile_rows(sigma, r, tile), factor_cols[0])
    product_full_0, diag_full_0 = reduce_and_gather(0, product_0[None])
    product_full_0 = product_full_0[0]
    diag_full_0 = diag_full_0[0]
    level_1 = []
    for node in (1, 2):
        slots = picks_all[node - 1]
        spread = scatter_factor(factor_cols[node], slots, positions, tile)
        top_row = jnp.concatenate(
            [
                -jnp.transpose(tile_cols(product_full_0, own_row, tile)),
                tile_rows(diag_full_0, own_row, tile),
            ],
            axis=1,
        )
        source = slots[jnp.maximum(r, own_tiles)]
        source_row = jnp.maximum(source, 0)
        low_row = jnp.concatenate(
            [tile_rows(sigma, source_row, tile), -tile_rows(product_full_0, source_row, tile)],
            axis=1,
        )
        low_row = jnp.where(source >= 0, low_row, 0.0)
        row = jnp.where(upper, top_row, low_row)
        level_1.append(mm(row, spread))
    product_1 = jnp.stack(level_1)
    product_full_1, diag_full_1 = reduce_and_gather(1, product_1)
    level_2 = []
    for node in range(3, nodes):
        slots = picks_all[node - 1]
        parent = parents[node - 3] - 1
        parent_slots = jnp.take(picks_all, parent, axis=0)
        product_p = jnp.take(product_full_1, parent, axis=0)
        diag_p = jnp.take(diag_full_1, parent, axis=0)
        spread = scatter_factor(factor_cols[node], slots, positions, tile)
        top_row = jnp.concatenate(
            [-jnp.transpose(tile_cols(product_p, own_row, tile)), tile_rows(diag_p, own_row, tile)],
            axis=1,
        )
        source = slots[jnp.maximum(r, own_tiles)]
        source_row = jnp.clip(source, 0, own_tiles - 1)
        corner = pick_transposed(
            -tile_cols(product_full_0, source_row, tile), parent_slots[own_tiles:], tile
        )
        low_row = jnp.concatenate(
            [
                tile_rows(diag_full_0, source_row, tile),
                corner,
                -tile_rows(product_p, source_row, tile),
            ],
            axis=1,
        )
        low_row = jnp.where(source >= 0, low_row, 0.0)
        row = jnp.where(upper, top_row, low_row)
        level_2.append(mm(row, spread))
    product_2 = jnp.stack(level_2)
    first_2 = 3
    count_2 = product_2.shape[0]
    gram_rows = jnp.zeros((count_2, width, tile), jnp.float32)
    gram_rows = lax.dynamic_update_slice_in_dim(
        gram_rows, gram_piece[first_2 : first_2 + count_2], r * band, 1
    )
    diag_2 = lax.psum(diag_partial(first_2, product_2) + gram_rows, "row")
    products = jnp.concatenate([product_0[None], product_1, product_2], axis=0)
    diag_cols = jnp.concatenate(
        [
            tile_cols(diag_full_0, c, tile)[None],
            lax.dynamic_slice_in_dim(diag_full_1, c * tile, tile, 2),
            diag_2,
        ],
        axis=0,
    )
    return ((-products)[None], diag_cols[None])


def solution(mesh):
    return jax.shard_map(
        body,
        mesh=mesh,
        in_specs=(
            P(("leaf", "row"), "col"),
            P("leaf", None, "row", "col"),
            P("leaf", None, "col", None),
            P("leaf", None, None),
            P("leaf", None),
        ),
        out_specs=(P("leaf", None, "row", "col"), P("leaf", None, None, "col")),
        check_vma=False,
    )
```

profile of v0, /device:TPU:0, one launch (start us, length us, event | category | flops | bytes accessed | tf_op | source)
XLA Modules:
  0.0 459.2 jit_solution(14943117877159287603)
XLA Ops:
  9.5 3.9 fusion.2
  14.3 57.6 %all-reduce.4.cloned.1.call-done = f32[7,128,512]{2,1,0:T(8,128)} async-done(((f32[7,128,512]{2,1,0:T(8,128)}), f32[7,128,512]{2,1,0:T(8,128)}) %all-reduce.4.cloned.1.call-update) | async-done | bytes 1835024 | tf_op jit(solution)/shard_map/psum | solution.py:57
  78.3 18.1 %all-gather.10.cloned.1.call-done = f32[4096,256]{1,0:T(8,128)} async-done(((f32[32,256]{1,0:T(8,128)}), f32[4096,256]{1,0:T(8,128)}) %all-gather.10.cloned.1.call-update) | async-done | bytes 4194320 | tf_op jit(solution)/shard_map/all_gather | solution.py:67
  96.3 5.8 %copy.83 = f32[32,4,32,256]{3,1,2,0:T(4,128)S(1)} copy(f32[32,4,32,256]{3,2,1,0:T(8,128)} %bitcast.194) | data formatting | bytes 8388608 | tf_op jit(solution)/shard_map/reshape | solution.py:68
  102.2 3.0 copy.124
  105.1 20.2 %all-gather.8.cloned.1.call-done = f32[7,1024,128]{2,1,0:T(8,128)} async-done(((f32[7,128,128]{2,1,0:T(8,128)}), f32[7,1024,128]{2,1,0:T(8,128)}) %all-gather.8.cloned.1.call-update) | async-done | bytes 3670032 | tf_op jit(solution)/shard_map/all_gather | solution.py:62
  129.2 30.5 %reduce-scatter.4.cloned.1.call-done = f32[1,64,128]{2,1,0:T(8,128)} async-done(((f32[1,512,128]{2,1,0:T(8,128)}), f32[1,64,128]{2,1,0:T(8,128)}) %reduce-scatter.4.cloned.1.call-update) | async-done | bytes 32784 | tf_op jit(solution)/shard_map/reduce_scatter | solution.py:79
  170.4 3.1 fusion.102
  182.0 23.9 %all-gather.12.cloned.1.call-done = f32[32,192,128]{2,1,0:T(8,128)} async-done(((f32[1,192,128]{2,1,0:T(8,128)}), f32[32,192,128]{2,1,0:T(8,128)}) %all-gather.12.cloned.1.call-update) | async-done | bytes 3145744 | tf_op jit(solution)/shard_map/all_gather | solution.py:84
  207.3 3.2 slice.189
  231.2 30.5 %reduce-scatter.8.cloned.1.call-done = f32[2,64,128]{2,1,0:T(8,128)} async-done(((f32[2,512,128]{2,1,0:T(8,128)}), f32[2,64,128]{2,1,0:T(8,128)}) %reduce-scatter.8.cloned.1.call-update) | async-done | bytes 65552 | tf_op jit(solution)/shard_map/reduce_scatter | solution.py:79
  299.2 12.6 %all-gather.14.cloned.1.call-done = f32[64,192,128]{2,1,0:T(8,128)} async-done(((f32[2,192,128]{2,1,0:T(8,128)}), f32[64,192,128]{2,1,0:T(8,128)}) %all-gather.14.cloned.1.call-update) | async-done | bytes 6291472 | tf_op jit(solution)/shard_map/all_gather | solution.py:84
  311.9 3.2 slice.195
  315.0 4.7 %slice.194 = f32[8,4,2,128,128]{4,3,2,1,0:T(8,128)} slice(f32[8,4,2,192,128]{4,3,2,1,0:T(8,128)} %bitcast.193), slice={[0:8], [0:4], [0:2], [0:128], [0:128]} | slice | bytes 8388608 | tf_op jit(solution)/shard_map/slice | solution.py:86
  319.8 5.3 %copy.118 = f32[8,4,2,128,128]{3,0,4,1,2:T(8,128)} copy(f32[8,4,2,128,128]{4,3,2,1,0:T(8,128)} %slice.194) | data formatting | bytes 8388608
  325.0 4.9 %reshape.293 = f32[2,1024,512]{1,2,0:T(8,128)} reshape(f32[2,8,128,4,128]{2,1,4,3,0:T(8,128)} %bitcast.183) | data formatting | bytes 8388608 | tf_op jit(solution)/shard_map/reshape | solution.py:86
  329.9 4.3 copy.134
  334.2 3.1 reshape.294
  337.3 4.2 select_bitcast_fusion.4
  345.8 7.9 %select_bitcast_fusion = (f32[1024,512]{0,1:T(8,128)}, f32[1,1024,512]{1,2,0:T(8,128)}, f32[1,1024,512]{1,2,0:T(8,128)}, f32[1,1024,512]{1,2,0:T(8,128)}) fusion(f32[2,1024,512]{1,2,0:T(8,128)} %reshape.293, s32[]{:T(128)S(6)} %select_n.346, pred[]{:T(512)S(6)} %and.78, s32[]{:T(128)S(6)} %select_n.326, s32[]{:T(128)S(6)} %select_n.316, s32[]{:T(128)S(6)} %select_n.336), kind=kLoop, calls=%fused_computation.12 | loop fusion | flops 524288 | bytes 16777232 | tf_op jit(solution)/shard_map/jit(_take)/select_n | solution.py:127
  363.7 3.0 copy.119
  370.6 2.9 copy.122
  377.5 3.3 bitcast_dynamic-update-slice_fusion.3
  391.4 57.6 %all-reduce.6.cloned.1.call-done = f32[4,512,128]{2,1,0:T(8,128)} async-done(((f32[4,512,128]{2,1,0:T(8,128)}), f32[4,512,128]{2,1,0:T(8,128)}) %all-reduce.6.cloned.1.call-update) | async-done | bytes 1048592 | tf_op jit(solution)/shard_map/psum | solution.py:157
  (225 shorter events, 116.0 us)
Async XLA Ops:
  8.0 6.0 %copy-start.37 = (s32[1,6,8]{2,0,1:T(1,128)S(1)}, s32[1,6,8]{2,0,1:T(1,128)}, u32[]{:S(2)}) copy-start(s32[1,6,8]{2,0,1:T(1,128)} %param.18) | copy-start | bytes 580
  8.0 63.9 %all-reduce.4.cloned.1.call-start = ((), (), s32[]{:S(2)}) async-start(), calls=%async_computation.3 | async-start | bytes 3670016 | tf_op jit(solution)/shard_map/psum | solution.py:57
  13.4 82.9 %all-gather.10.cloned.1.call-start = ((), (), s32[]{:S(2)}) async-start(), calls=%async_computation.9 | async-start | bytes 4227072 | tf_op jit(solution)/shard_map/all_gather | solution.py:67
  14.0 111.3 %all-gather.8.cloned.1.call-start = ((), (), s32[]{:S(2)}) async-start(), calls=%async_computation.4 | async-start | bytes 4128768 | tf_op jit(solution)/shard_map/all_gather | solution.py:62
  75.8 53.4 %reduce-scatter.6.cloned.1.call-start = ((), (), s32[]{:S(2)}) async-start(), calls=%async_computation.6 | async-start | bytes 1146880 | tf_op jit(solution)/shard_map/reduce_scatter | solution.py:65
  78.2 81.5 %reduce-scatter.4.cloned.1.call-start = ((), (), s32[]{:S(2)}) async-start(), calls=%async_computation.5 | async-start | bytes 294912 | tf_op jit(solution)/shard_map/reduce_scatter | solution.py:79
  102.1 25.6 %copy-start.3 = (f32[7,128,512]{2,1,0:T(8,128)S(1)}, f32[7,128,512]{2,1,0:T(8,128)}, u32[]{:S(2)}) copy-start(f32[7,128,512]{2,1,0:T(8,128)} %copy-done.2) | copy-start | bytes 5505028
  129.1 76.9 %all-gather.12.cloned.1.call-start = ((), (), s32[]{:S(2)}) async-start(), calls=%async_computation.10 | async-start | bytes 3244032 | tf_op jit(solution)/shard_map/all_gather | solution.py:84
  161.2 100.5 %reduce-scatter.8.cloned.1.call-start = ((), (), s32[]{:S(2)}) async-start(), calls=%async_computation.7 | async-start | bytes 589824 | tf_op jit(solution)/shard_map/reduce_scatter | solution.py:79
  229.4 34.2 %copy-start.38 = (s32[1,4]{1,0:T(1,128)S(1)}, s32[1,4]{1,0:T(1,128)}, u32[]{:S(2)}) copy-start(s32[1,4]{1,0:T(1,128)} %param.19) | copy-start | bytes 52
  229.4 47.4 %copy-start.7 = (f32[1,1024,128]{2,1,0:T(8,128)S(1)}, f32[1,1024,128]{2,1,0:T(8,128)}, u32[]{:S(2)}) copy-start(f32[1,1024,128]{2,1,0:T(8,128)} %get-tuple-element.69) | copy-start | bytes 1572868
  231.2 47.1 %copy-start.6 = (f32[1,1024,128]{2,1,0:T(8,128)S(1)}, f32[1,1024,128]{2,1,0:T(8,128)}, u32[]{:S(2)}) copy-start(f32[1,1024,128]{2,1,0:T(8,128)} %get-tuple-element.71) | copy-start | bytes 1572868
  231.2 80.7 %all-gather.14.cloned.1.call-start = ((), (), s32[]{:S(2)}) async-start(), calls=%async_computation.11 | async-start | bytes 6488064 | tf_op jit(solution)/shard_map/all_gather | solution.py:84
  263.3 185.8 %all-reduce.6.cloned.1.call-start = ((), (), s32[]{:S(2)}) async-start(), calls=%async_computation.8 | async-start | bytes 2097152 | tf_op jit(solution)/shard_map/psum | solution.py:157
  283.8 6.0 %copy-start.19 = (f32[1024,128]{0,1:T(8,128)S(1)}, f32[1024,128]{0,1:T(8,128)}, u32[]{:S(2)}) copy-start(f32[1024,128]{0,1:T(8,128)} %get-tuple-element.76) | copy-start | bytes 1572868
  285.9 7.6 %copy-start.18 = (f32[1024,128]{0,1:T(8,128)S(1)}, f32[1024,128]{0,1:T(8,128)}, u32[]{:S(2)}) copy-start(f32[1024,128]{0,1:T(8,128)} %get-tuple-element.77) | copy-start | bytes 1572868
  290.8 6.0 %copy-start.17 = (f32[1024,128]{0,1:T(8,128)S(1)}, f32[1024,128]{0,1:T(8,128)}, u32[]{:S(2)}) copy-start(f32[1024,128]{0,1:T(8,128)} %get-tuple-element.78) | copy-start | bytes 1572868
  293.7 4.9 %copy-start.22 = (f32[1024,128]{1,0:T(8,128)S(1)}, f32[1024,128]{1,0:T(8,128)}, u32[]{:S(2)}) copy-start(f32[1024,128]{1,0:T(8,128)} %copy.108) | copy-start | bytes 1572868
  377.4 5.0 %copy-start.9 = (f32[128,1536]{1,0:T(8,128)S(1)}, f32[128,1536]{1,0:T(8,128)}, u32[]{:S(2)}) copy-start(f32[128,1536]{1,0:T(8,128)} %copy.106) | copy-start | bytes 2359300
  377.4 5.0 %copy-start.14 = (f32[12,128,128]{2,1,0:T(8,128)S(1)}, f32[12,128,128]{2,1,0:T(8,128)}, u32[]{:S(2)}) copy-start(f32[12,128,128]{2,1,0:T(8,128)} %select_select_fusion.1) | copy-start | bytes 2359300
  377.4 5.0 %copy-start.23 = (f32[128,512]{1,0:T(8,128)S(1)}, f32[128,512]{1,0:T(8,128)}, u32[]{:S(2)}) copy-start(f32[128,512]{1,0:T(8,128)} %get-tuple-element.87) | copy-start | bytes 786436
  377.4 5.0 %copy-start.27 = (f32[128,512]{1,0:T(8,128)S(1)}, f32[128,512]{1,0:T(8,128)}, u32[]{:S(2)}) copy-start(f32[128,512]{1,0:T(8,128)} %dynamic-slice_negate_fusion.5) | copy-start | bytes 786436
  377.4 5.0 %copy-start.28 = (f32[128,512]{1,0:T(8,128)S(1)}, f32[128,512]{1,0:T(8,128)}, u32[]{:S(2)}) copy-start(f32[128,512]{1,0:T(8,128)} %copy.105) | copy-start | bytes 786436
  390.2 61.4 %copy-start.1 = (f32[1,7,128,512]{3,2,1,0:T(8,128)S(1)}, f32[1,7,128,512]{3,2,1,0:T(8,128)}, u32[]{:S(2)}) copy-start(f32[1,7,128,512]{3,2,1,0:T(8,128)} %param.17) | copy-start | bytes 5505028
  (24 other events, 68.5 us)
Sparse Core Ops, SparseCore 0:
  13.5 58.3 all-reduce.3
  79.1 22.6 reduce-scatter.5
  129.2 30.4 reduce-scatter.3
  162.1 43.8 all-gather.11
  231.3 30.3 reduce-scatter.7
  263.8 48.0 all-gather.13
Sparse Core Ops, SparseCore 1:
  17.0 79.3 all-gather.9
  98.5 26.8 all-gather.7
  388.5 60.5 all-reduce.5
where the time goes:
time: 461 us; the launch traced here: 459 us
  waiting for transfers between devices  252 us (55%)
  local copies, waits for them, and re-layouts  100 us (22%)
  other arithmetic  53.9 us (12%)
  between operations  26.5 us (6%)
  matrix products  26 us (6%)
    reduce_scatter x2, waiting for transfers between devices, reduce_and_gather(): lax.psum_scatter(diag_partial(first, products), 'row', scatter_dimension=...  61 us
    psum x1, waiting for transfers between devices, body(): factor_rows = lax.psum(partial_factor, 'col')  57.6 us
    psum x1, waiting for transfers between devices, body(): diag_2 = lax.psum(diag_partial(first_2, product_2) + gram_rows, 'row')  57.6 us
    all_gather x2, waiting for transfers between devices, reduce_and_gather(): everything = lax.all_gather(both, ('row', 'col'), axis=0)  36.5 us
    unnamed x92, local copies, waits for them, and re-layouts  35.4 us
    dot_general x12, matrix products, mm(): jnp.matmul(a, b, precision=HIGHEST, preferred_element_type=jnp.float32)  26 us
    all_gather x1, waiting for transfers between devices, body(): factor_cols = lax.all_gather(factor_tile, 'row', axis=1, tiled=True)  20.2 us
    all_gather x1, waiting for transfers between devices, body(): gathered = lax.all_gather(sigma_top, ('leaf', 'row', 'col'), axis=0)  18.1 us
  transfers between devices with their start and end apart: 9, of which 8 were waited for; matrix products, arithmetic and copies ran while one was open for 15% of the time, Pallas kernels for 0%

commit v1 on v0

--- a/solution.py
+++ b/solution.py
@@ -59,7 +59,9 @@
     live_here = jnp.take(living, r, axis=1).astype(jnp.float32)
     factor_rows = factor_rows * live_here[:, None, None]
     factor_tile = lax.dynamic_slice_in_dim(factor_rows, c * tile, tile, 2)
-    factor_cols = lax.all_gather(factor_tile, "row", axis=1, tiled=True)
+    factor_cols = jnp.concatenate(
+        lax.all_to_all(jnp.stack([factor_tile] * lax.axis_size("row")), "row", 0, 0), axis=1
+    )
     inverse_band = lax.dynamic_slice_in_dim(inverse, r * band, band, 2)
     partial_gram = mm(jnp.transpose(inverse_band, (0, 2, 1)), inverse)
     gram_piece = lax.psum_scatter(partial_gram, "col", scatter_dimension=2, tiled=True)

time: 461 us -> 474 us (1.028)
  waiting for transfers between devices: 252 us -> 260 us
    all_to_all x0 -> x1, waiting for transfers between devices: none -> 44.6 us  [body(): lax.all_to_all(jnp.stack([factor_tile] * lax.axis_size('row')), 'row', 0, 0)]
    all_gather x1 -> x0, waiting for transfers between devices: 20.2 us -> none  [body(): factor_cols = lax.all_gather(factor_tile, 'row', axis=1, tiled=True)]
    all_gather x1, waiting for transfers between devices: 18.1 us -> 0.01 us  [body(): gathered = lax.all_gather(sigma_top, ('leaf', 'row', 'col'), axis=0)]
    another operation x0 -> x2, local copies, waits for them, and re-layouts: none -> 5.87 us  [the longest x1 3.48 us: scatter_factor(): tiles = factor_col.reshape(slots.shape[0], tile, factor_col.shape[1])]
    unnamed x92 -> x96, local copies, waits for them, and re-layouts: 35.4 us -> 35.4 us
  transfers between devices with their start and end apart: 9 -> 9, of which waited for: 8 -> 7; matrix products, arithmetic and copies ran while one was open for 15% -> 14% of each run, Pallas kernels for 0% -> 0%
where the time goes in v1:
time: 474 us; the launch traced here: 473 us
  waiting for transfers between devices  260 us (55%)
  local copies, waits for them, and re-layouts  102 us (22%)
  other arithmetic  53.7 us (11%)
  between operations  26.5 us (6%)
  matrix products  24.7 us (5%)
  starting transfers between devices  5.23 us (1%)
    reduce_scatter x2, waiting for transfers between devices, reduce_and_gather(): lax.psum_scatter(diag_partial(first, products), 'row', scatter_dimension=...  59.6 us
    psum x1, waiting for transfers between devices, body(): diag_2 = lax.psum(diag_partial(first_2, product_2) + gram_rows, 'row')  57.9 us
    psum x1, waiting for transfers between devices, body(): factor_rows = lax.psum(partial_factor, 'col')  57.7 us
    all_to_all x1, waiting for transfers between devices, body(): lax.all_to_all(jnp.stack([factor_tile] * lax.axis_size('row')), 'row', 0, 0)  44.6 us
    all_gather x2, waiting for transfers between devices, reduce_and_gather(): everything = lax.all_gather(both, ('row', 'col'), axis=0)  39.8 us
    unnamed x96, local copies, waits for them, and re-layouts  35.4 us
    dot_general x12, matrix products, mm(): jnp.matmul(a, b, precision=HIGHEST, preferred_element_type=jnp.float32)  24.7 us
    select_n x4, other arithmetic, body(): product_p = jnp.take(product_full_1, parent, axis=0)  13.4 us
  transfers between devices with their start and end apart: 9, of which 7 were waited for; matrix products, arithmetic and copies ran while one was open for 14% of the time, Pallas kernels for 0%

profile of v1, /device:TPU:0, one launch (start us, length us, event | category | flops | bytes accessed | tf_op | source)
XLA Modules:
  0.0 472.5 jit_solution(10889573823009870715)
XLA Ops:
  9.5 3.9 fusion.2
  14.3 57.7 %all-reduce.4.cloned.1.call-done = f32[7,128,512]{2,1,0:T(8,128)} async-done(((f32[7,128,512]{2,1,0:T(8,128)}), f32[7,128,512]{2,1,0:T(8,128)}) %all-reduce.4.cloned.1.call-update) | async-done | bytes 1835024 | tf_op jit(solution)/shard_map/psum | solution.py:57
  77.4 4.5 all-to-all-start
  84.3 44.6 %all-to-all-done = f32[8,7,128,128]{3,2,1,0:T(8,128)} async-done(((f32[8,7,128,128]{3,2,1,0:T(8,128)}), f32[8,7,128,128]{3,2,1,0:T(8,128)}, u32[]{:S(2)}, u32[]{:S(2)}) %all-to-all-start) | async-done | bytes 3670048 | tf_op jit(solution)/shard_map/all_to_all | solution.py:63
  128.8 3.5 slice_bitcast_fusion
  132.3 5.8 %copy.83 = f32[32,4,32,256]{3,1,2,0:T(4,128)S(1)} copy(f32[32,4,32,256]{3,2,1,0:T(8,128)} %bitcast.198) | data formatting | bytes 8388608 | tf_op jit(solution)/shard_map/reshape | solution.py:70
  143.7 29.1 %reduce-scatter.4.cloned.1.call-done = f32[1,64,128]{2,1,0:T(8,128)} async-done(((f32[1,512,128]{2,1,0:T(8,128)}), f32[1,64,128]{2,1,0:T(8,128)}) %reduce-scatter.4.cloned.1.call-update) | async-done | bytes 32784 | tf_op jit(solution)/shard_map/reduce_scatter | solution.py:81
  192.0 27.2 %all-gather.9.cloned.1.call-done = f32[32,192,128]{2,1,0:T(8,128)} async-done(((f32[1,192,128]{2,1,0:T(8,128)}), f32[32,192,128]{2,1,0:T(8,128)}) %all-gather.9.cloned.1.call-update) | async-done | bytes 3145744 | tf_op jit(solution)/shard_map/all_gather | solution.py:86
  220.5 3.2 slice.196
  244.4 30.5 %reduce-scatter.8.cloned.1.call-done = f32[2,64,128]{2,1,0:T(8,128)} async-done(((f32[2,512,128]{2,1,0:T(8,128)}), f32[2,64,128]{2,1,0:T(8,128)}) %reduce-scatter.8.cloned.1.call-update) | async-done | bytes 65552 | tf_op jit(solution)/shard_map/reduce_scatter | solution.py:81
  312.4 12.7 %all-gather.11.cloned.1.call-done = f32[64,192,128]{2,1,0:T(8,128)} async-done(((f32[2,192,128]{2,1,0:T(8,128)}), f32[64,192,128]{2,1,0:T(8,128)}) %all-gather.11.cloned.1.call-update) | async-done | bytes 6291472 | tf_op jit(solution)/shard_map/all_gather | solution.py:86
  325.1 3.2 slice.202
  328.3 4.7 %slice.201 = f32[8,4,2,128,128]{4,3,2,1,0:T(8,128)} slice(f32[8,4,2,192,128]{4,3,2,1,0:T(8,128)} %bitcast.197), slice={[0:8], [0:4], [0:2], [0:128], [0:128]} | slice | bytes 8388608 | tf_op jit(solution)/shard_map/slice | solution.py:88
  333.0 5.3 %copy.118 = f32[8,4,2,128,128]{3,0,4,1,2:T(8,128)} copy(f32[8,4,2,128,128]{4,3,2,1,0:T(8,128)} %slice.201) | data formatting | bytes 8388608
  338.2 4.9 %reshape.314 = f32[2,1024,512]{1,2,0:T(8,128)} reshape(f32[2,8,128,4,128]{2,1,4,3,0:T(8,128)} %bitcast.187) | data formatting | bytes 8388608 | tf_op jit(solution)/shard_map/reshape | solution.py:88
  343.1 4.3 copy.134
  347.5 3.1 reshape.315
  350.6 4.2 select_bitcast_fusion.4
  359.0 7.9 %select_bitcast_fusion = (f32[1024,512]{0,1:T(8,128)}, f32[1,1024,512]{1,2,0:T(8,128)}, f32[1,1024,512]{1,2,0:T(8,128)}, f32[1,1024,512]{1,2,0:T(8,128)}) fusion(f32[2,1024,512]{1,2,0:T(8,128)} %reshape.314, s32[]{:T(128)S(6)} %select_n.346, pred[]{:T(512)S(6)} %and.78, s32[]{:T(128)S(6)} %select_n.326, s32[]{:T(128)S(6)} %select_n.316, s32[]{:T(128)S(6)} %select_n.336), kind=kLoop, calls=%fused_computation.12 | loop fusion | flops 524288 | bytes 16777232 | tf_op jit(solution)/shard_map/jit(_take)/select_n | solution.py:129
  366.8 2.9 copy.121
  376.9 3.0 copy.119
  383.8 2.9 copy.122
  390.7 3.3 bitcast_dynamic-update-slice_fusion.3
  404.7 57.9 %all-reduce.6.cloned.1.call-done = f32[4,512,128]{2,1,0:T(8,128)} async-done(((f32[4,512,128]{2,1,0:T(8,128)}), f32[4,512,128]{2,1,0:T(8,128)}) %all-reduce.6.cloned.1.call-update) | async-done | bytes 1048592 | tf_op jit(solution)/shard_map/psum | solution.py:159
  (229 shorter events, 116.1 us)
Async XLA Ops:
  8.0 6.0 %copy-start.39 = (s32[1,6,8]{2,0,1:T(1,128)S(1)}, s32[1,6,8]{2,0,1:T(1,128)}, u32[]{:S(2)}) copy-start(s32[1,6,8]{2,0,1:T(1,128)} %param.18) | copy-start | bytes 580
  8.0 63.9 %all-reduce.4.cloned.1.call-start = ((), (), s32[]{:S(2)}) async-start(), calls=%async_computation.4 | async-start | bytes 3670016 | tf_op jit(solution)/shard_map/psum | solution.py:57
  13.4 118.9 %all-gather.7.cloned.1.call-start = ((), (), s32[]{:S(2)}) async-start(), calls=%async_computation.9 | async-start | bytes 4227072 | tf_op jit(solution)/shard_map/all_gather | solution.py:69
  77.4 51.4 %all-to-all-start = ((f32[8,7,128,128]{3,2,1,0:T(8,128)}), f32[8,7,128,128]{3,2,1,0:T(8,128)}, u32[]{:S(2)}, u32[]{:S(2)}) async-start(f32[8,7,128,128]{3,2,1,0:T(8,128)} %stack.35), calls=%async_computation | async-start | bytes 7340032 | tf_op jit(solution)/shard_map/all_to_all | solution.py:63
  81.9 61.8 %reduce-scatter.6.cloned.1.call-start = ((), (), s32[]{:S(2)}) async-start(), calls=%async_computation.6 | async-start | bytes 1146880 | tf_op jit(solution)/shard_map/reduce_scatter | solution.py:67
  84.2 88.7 %reduce-scatter.4.cloned.1.call-start = ((), (), s32[]{:S(2)}) async-start(), calls=%async_computation.5 | async-start | bytes 294912 | tf_op jit(solution)/shard_map/reduce_scatter | solution.py:81
  138.1 4.3 copy-start.3
  143.7 75.5 %all-gather.9.cloned.1.call-start = ((), (), s32[]{:S(2)}) async-start(), calls=%async_computation.10 | async-start | bytes 3244032 | tf_op jit(solution)/shard_map/all_gather | solution.py:86
  174.3 100.5 %reduce-scatter.8.cloned.1.call-start = ((), (), s32[]{:S(2)}) async-start(), calls=%async_computation.7 | async-start | bytes 589824 | tf_op jit(solution)/shard_map/reduce_scatter | solution.py:81
  242.5 34.2 %copy-start.40 = (s32[1,4]{1,0:T(1,128)S(1)}, s32[1,4]{1,0:T(1,128)}, u32[]{:S(2)}) copy-start(s32[1,4]{1,0:T(1,128)} %param.19) | copy-start | bytes 52
  242.5 47.4 %copy-start.8 = (f32[8,128,128]{2,1,0:T(8,128)S(1)}, f32[8,128,128]{2,1,0:T(8,128)}, u32[]{:S(2)}) copy-start(f32[8,128,128]{2,1,0:T(8,128)} %get-tuple-element.70) | copy-start | bytes 1572868
  244.3 47.1 %copy-start.7 = (f32[8,128,128]{2,1,0:T(8,128)S(1)}, f32[8,128,128]{2,1,0:T(8,128)}, u32[]{:S(2)}) copy-start(f32[8,128,128]{2,1,0:T(8,128)} %get-tuple-element.71) | copy-start | bytes 1572868
  244.4 80.7 %all-gather.11.cloned.1.call-start = ((), (), s32[]{:S(2)}) async-start(), calls=%async_computation.11 | async-start | bytes 6488064 | tf_op jit(solution)/shard_map/all_gather | solution.py:86
  276.4 186.1 %all-reduce.6.cloned.1.call-start = ((), (), s32[]{:S(2)}) async-start(), calls=%async_computation.8 | async-start | bytes 2097152 | tf_op jit(solution)/shard_map/psum | solution.py:159
  297.0 6.0 %copy-start.21 = (f32[1024,128]{0,1:T(8,128)S(1)}, f32[1024,128]{0,1:T(8,128)}, u32[]{:S(2)}) copy-start(f32[1024,128]{0,1:T(8,128)} %get-tuple-element.77) | copy-start | bytes 1572868
  299.1 7.5 %copy-start.20 = (f32[1024,128]{0,1:T(8,128)S(1)}, f32[1024,128]{0,1:T(8,128)}, u32[]{:S(2)}) copy-start(f32[1024,128]{0,1:T(8,128)} %get-tuple-element.78) | copy-start | bytes 1572868
  304.0 6.0 %copy-start.19 = (f32[1024,128]{0,1:T(8,128)S(1)}, f32[1024,128]{0,1:T(8,128)}, u32[]{:S(2)}) copy-start(f32[1024,128]{0,1:T(8,128)} %get-tuple-element.79) | copy-start | bytes 1572868
  306.8 4.9 %copy-start.24 = (f32[1024,128]{1,0:T(8,128)S(1)}, f32[1024,128]{1,0:T(8,128)}, u32[]{:S(2)}) copy-start(f32[1024,128]{1,0:T(8,128)} %copy.108) | copy-start | bytes 1572868
  390.6 5.0 %copy-start.10 = (f32[128,1536]{1,0:T(8,128)S(1)}, f32[128,1536]{1,0:T(8,128)}, u32[]{:S(2)}) copy-start(f32[128,1536]{1,0:T(8,128)} %copy.106) | copy-start | bytes 2359300
  390.6 5.0 %copy-start.15 = (f32[12,128,128]{2,1,0:T(8,128)S(1)}, f32[12,128,128]{2,1,0:T(8,128)}, u32[]{:S(2)}) copy-start(f32[12,128,128]{2,1,0:T(8,128)} %select_select_fusion.1) | copy-start | bytes 2359300
  390.7 5.0 %copy-start.25 = (f32[128,512]{1,0:T(8,128)S(1)}, f32[128,512]{1,0:T(8,128)}, u32[]{:S(2)}) copy-start(f32[128,512]{1,0:T(8,128)} %get-tuple-element.88) | copy-start | bytes 786436
  390.7 5.0 %copy-start.29 = (f32[128,512]{1,0:T(8,128)S(1)}, f32[128,512]{1,0:T(8,128)}, u32[]{:S(2)}) copy-start(f32[128,512]{1,0:T(8,128)} %dynamic-slice_negate_fusion.5) | copy-start | bytes 786436
  390.7 5.0 %copy-start.30 = (f32[128,512]{1,0:T(8,128)S(1)}, f32[128,512]{1,0:T(8,128)}, u32[]{:S(2)}) copy-start(f32[128,512]{1,0:T(8,128)} %copy.105) | copy-start | bytes 786436
  403.4 61.7 %copy-start.1 = (f32[1,7,128,512]{3,2,1,0:T(8,128)S(1)}, f32[1,7,128,512]{3,2,1,0:T(8,128)}, u32[]{:S(2)}) copy-start(f32[1,7,128,512]{3,2,1,0:T(8,128)} %param.17) | copy-start | bytes 5505028
  (26 other events, 73.4 us)
Sparse Core Ops, SparseCore 0:
  13.5 58.3 all-reduce.3
  85.2 23.0 reduce-scatter.5
  143.8 29.0 reduce-scatter.3
  175.2 43.8 all-gather.8
  244.5 30.3 reduce-scatter.7
  277.0 48.0 all-gather.10
  401.8 60.7 all-reduce.5
Sparse Core Ops, SparseCore 1:
  17.0 80.5 all-gather.6
